TPU v7x, 32 devices: a whole 2x2x4 slice. The times are simulated.
32 devices in a mesh: row: 4 (over z), col: 8 (over y, x, core).
Axes of the slice: x: 2, y: 2, z: 4, core: 2. Of those that a mesh axis runs over, the one named last changes fastest.
Arguments:
- right_side: float32 [2, 16, 512, 512], P(None, None, 'row', 'col'), may hold values from -12 to 12
- symbol: float32 [1024, 1024, 256], P('col', 'row'), may hold values from -0.25 to 4.75, as said below
Outputs:
- solution_field: float32 [2, 16, 512, 512], P(None, None, 'row', 'col')
- residual: float32 [2, 16, 512, 512], P(None, None, 'row', 'col')
Inputs may be any that keep to these rules, and one draw needn't show every extreme that they name: For each frequency pair (u, v) the 16 x 16 matrix with entries symbol[u, v, s * 16 + t] is symmetric and positive definite.
All inputs are finite; a program needn't handle non-finite values.
Results may differ from a plain program's by a relative error of at most 0.0003.
Values sent between devices are 32-bit elements; how exact they have to be, the bound alone decides.
A program may use at most 576 MiB of HBM per device.

v0:
```python
import math
import jax
import jax.numpy as jnp
from jax import lax
from jax.sharding import PartitionSpec as P

precise = lax.Precision.HIGHEST


def twiddle(out_index, in_index, length):
    product = out_index[:, None] * in_index[None, :] % length
    angle = product.astype(jnp.float32) * (2.0 * math.pi / length)
    return (jnp.cos(angle), jnp.sin(angle))


def widen(values):
    return values[:, None, None, None]


def squares(residual):
    return lax.psum(jnp.sum(residual * residual, axis=(1, 2, 3)), ("row", "col"))


def local(right_side, symbol):
    row_count = lax.axis_size("row")
    col_count = lax.axis_size("col")
    rhs_count, seg_count, row_block, col_block = right_side.shape
    rows_all = row_block * row_count
    cols_all = col_block * col_count
    freq_rows = 2 * rows_all
    freq_cols = 2 * cols_all
    blocks = symbol.reshape(symbol.shape[0], symbol.shape[1], seg_count, seg_count)
    rows_cos, rows_sin = twiddle(
        jnp.arange(freq_rows, dtype=jnp.int32), jnp.arange(rows_all, dtype=jnp.int32), freq_rows
    )
    cols_cos, cols_sin = twiddle(
        jnp.arange(freq_cols, dtype=jnp.int32), jnp.arange(cols_all, dtype=jnp.int32), freq_cols
    )
    back_cols_cos, back_cols_sin = (cols_cos.T, cols_sin.T)
    back_rows_cos, back_rows_sin = (rows_cos.T, rows_sin.T)
    norm_factor = 1.0 / (freq_rows * freq_cols)
    residual = right_side
    norm_now = squares(residual)
    whole_rows = lax.all_to_all(right_side, "row", split_axis=1, concat_axis=2, tiled=True)
    real_rows = jnp.einsum("ui,ksij->ksuj", rows_cos, whole_rows, precision=precise)
    imag_rows = -jnp.einsum("ui,ksij->ksuj", rows_sin, whole_rows, precision=precise)
    whole_cols = lax.all_to_all(
        jnp.stack([real_rows, imag_rows]), "col", split_axis=3, concat_axis=4, tiled=True
    )
    cos_part = jnp.einsum("vj,rksuj->rksuv", cols_cos, whole_cols, precision=precise)
    sin_part = jnp.einsum("vj,rksuj->rksuv", cols_sin, whole_cols, precision=precise)
    spectrum = jnp.stack([cos_part[0] + sin_part[1], cos_part[1] - sin_part[0]])
    all_segments = lax.all_to_all(spectrum, "row", split_axis=4, concat_axis=2, tiled=True)
    mixture = jnp.einsum("uvst,rktuv->rksuv", blocks, all_segments, precision=precise)
    own_segments = lax.all_to_all(mixture, "row", split_axis=2, concat_axis=4, tiled=True)
    cos_back = jnp.einsum("jv,rksuv->rksuj", back_cols_cos, own_segments, precision=precise)
    sin_back = jnp.einsum("jv,rksuv->rksuj", back_cols_sin, own_segments, precision=precise)
    inverted = jnp.stack([cos_back[0] - sin_back[1], sin_back[0] + cos_back[1]])
    freq_whole = lax.all_to_all(inverted, "col", split_axis=4, concat_axis=3, tiled=True)
    spatial = jnp.einsum("iu,ksuj->ksij", back_rows_cos, freq_whole[0], precision=precise)
    spatial = (
        spatial - jnp.einsum("iu,ksuj->ksij", back_rows_sin, freq_whole[1], precision=precise)
    ) * norm_factor
    returned = lax.all_to_all(spatial, "row", split_axis=2, concat_axis=1, tiled=True)
    curve = lax.psum(jnp.sum(right_side * returned, axis=(1, 2, 3)), ("row", "col"))
    step_size = widen(norm_now / curve)
    solution = step_size * right_side
    residual = residual - step_size * returned
    return (solution, residual)


def solution(mesh):
    placed = (P(None, None, "row", "col"), P("col", "row", None))
    return jax.shard_map(
        local,
        mesh=mesh,
        in_specs=placed,
        out_specs=(P(None, None, "row", "col"), P(None, None, "row", "col")),
        check_vma=False,
    )
```

profile of v0, /device:TPU:0, one launch (start us, length us, event | category | flops | bytes accessed | tf_op | source)
XLA Modules:
  0.0 1495.4 jit_solution(2727610797402067509)
XLA Ops:
  0.6 1.3 copy.43
  2.0 31.9 %all_to_all.105 = f32[2,16,128,64]{2,3,0,1:T(8,128)S(1)} all-to-all(f32[2,16,128,64]{2,3,0,1:T(8,128)S(1)} %copy.43), channel_id=1, replica_groups=mesh['row'=4,'col'=8] {'row'}, dimensions={1} | all-to-all | bytes 2097152 | tf_op jit(solution)/shard_map/all_to_all | solution.py:44
  33.8 0.7 copy.78
  34.5 0.4 all_to_all.79
  34.9 12.5 negate_bitcast_fusion
  47.5 12.7 fusion.24
  60.2 2.3 pad_maximum_fusion.1
  62.5 8.6 copy.45
  71.0 11.5 reshape.18
  82.5 53.7 %all_to_all.106 = f32[8,1,131072]{2,1,0:T(1,128)} all-to-all(f32[8,1,131072]{2,1,0:T(1,128)} %reshape.18), channel_id=1, replica_groups=mesh['row'=4,'col'=8] {'col'}, dimensions={0} | all-to-all | bytes 8388608 | tf_op jit(solution)/shard_map/all_to_all | solution.py:47
  136.3 0.5 broadcast.73
  136.8 13.7 reduce
  150.5 11.1 reshape.19
  161.6 8.5 copy.73
  170.1 0.0 copy-start.2
  170.1 38.7 %fusion.17 = f32[2,2,4,128,1024]{4,3,2,1,0:T(8,128)} fusion(f32[2,2,4,128,512]{3,4,2,1,0:T(8,128)} %bitcast.111), kind=kOutput, calls=%fused_computation.28 | convolution fusion | flops 12892241920 | bytes 12582912 | tf_op jit(solution)/shard_map/vj,rksuj->rksuv/dot_general | solution.py:51
  208.9 0.0 copy-done.2
  208.9 36.0 %fusion.5 = f32[2,2,4,128,1024]{4,3,2,1,0:T(8,128)} fusion(f32[2,2,4,128,512]{3,4,2,1,0:T(8,128)S(1)} %bitcast.112), kind=kOutput, calls=%fused_computation.16 | convolution fusion | flops 12892241920 | bytes 12582912 | tf_op jit(solution)/shard_map/vj,rksuj->rksuv/dot_general | solution.py:50
  244.9 10.3 slice_add_fusion
  255.2 6.7 pad_maximum_fusion
  261.9 10.2 copy.50
  272.1 5.6 all-to-all-start.2
  277.7 33.5 %copy.53 = f32[128,256,256]{1,2,0:T(8,128)} copy(f32[128,256,256]{2,1,0:T(8,128)} %param.3) | data formatting | bytes 67108864 | tf_op args[1]
  311.2 124.5 %copy.71 = f32[128,256,16,16,1]{3,2,4,1,0:T(8,128)} copy(f32[128,256,16,16,1]{1,3,2,0,4:T(8,128)} %bitcast.100) | data formatting | bytes 67108864 | tf_op jit(solution)/shard_map/reshape | solution.py:32
  435.6 24.8 %all-to-all-done.2 = f32[2,2,4,128,1024]{3,2,1,0,4:T(4,128)} async-done(((f32[2,2,4,128,1024]{3,2,1,0,4:T(4,128)}), f32[2,2,4,128,1024]{3,2,1,0,4:T(4,128)}, u32[]{:S(2)}, u32[]{:S(2)}) %all-to-all-start.2) | async-done | bytes 8388640 | tf_op jit(solution)/shard_map/all_to_all | solution.py:53
  460.5 9.3 copy.51
  469.8 9.9 copy.52
  479.7 52.4 %copy.54 = f32[2,2,16,128,256]{2,1,0,4,3:T(2,128)} copy(f32[2,2,16,128,256]{4,3,2,1,0:T(8,128)} %bitcast.101) | data formatting | bytes 16777216 | tf_op jit(solution)/shard_map/all_to_all | solution.py:53
  532.1 443.6 %convolution_bitcast_fusion = f32[2,2,16,128,256]{2,1,0,4,3:T(2,128)} fusion(f32[2,2,16,128,256]{2,1,0,4,3:T(2,128)} %copy.54, f32[128,256,16,16,1]{3,2,4,1,0:T(8,128)} %copy.71), kind=kOutput, calls=%fused_computation | convolution fusion | flops 402653184 | bytes 50331648 | tf_op jit(solution)/shard_map/uvst,rktuv->rksuv/dot_general | solution.py:54
  975.7 54.4 %copy.56 = f32[2,2,16,128,256]{4,3,1,0,2:T(8,128)} copy(f32[2,2,16,128,256]{2,1,0,4,3:T(2,128)} %convolution_bitcast_fusion) | data formatting | bytes 16777216 | tf_op jit(solution)/shard_map/uvst,rktuv->rksuv/transpose | solution.py:54
  1030.1 190.1 %all_to_all.107 = f32[2,2,16,128,256]{4,3,1,0,2:T(8,128)} all-to-all(f32[2,2,16,128,256]{4,3,1,0,2:T(8,128)} %copy.56), channel_id=1, replica_groups=mesh['row'=4,'col'=8] {'row'}, dimensions={2} | all-to-all | bytes 16777216 | tf_op jit(solution)/shard_map/all_to_all | solution.py:55
  1220.2 12.2 copy.58
  1232.3 10.7 all_to_all.91
  1243.1 0.0 copy-start.1
  1243.1 52.4 %fusion.15 = f32[2,2,4,128,512]{4,3,2,1,0:T(8,128)S(1)} fusion(f32[2,2,4,128,1024]{4,3,2,1,0:T(8,128)} %all_to_all.91), kind=kOutput, calls=%fused_computation.26 | convolution fusion | flops 12892241920 | bytes 12582912 | tf_op jit(solution)/shard_map/jv,rksuv->rksuj/dot_general | solution.py:57
  1295.5 0.0 copy-done.1
  1295.5 22.5 %fusion.3 = f32[2,2,4,128,512]{4,3,2,1,0:T(8,128)S(1)} fusion(f32[2,2,4,128,1024]{4,3,2,1,0:T(8,128)S(1)} %copy-done.1), kind=kOutput, calls=%fused_computation.14 | convolution fusion | flops 12892241920 | bytes 12582912 | tf_op jit(solution)/shard_map/jv,rksuv->rksuj/dot_general | solution.py:56
  1318.1 1.0 slice_subtract_fusion.1
  1319.1 2.4 pad_maximum_fusion.2
  1321.5 5.4 copy.59
  1326.9 52.9 %all_to_all.108 = f32[2,2,4,128,512]{3,2,1,0,4:T(4,128)S(1)} all-to-all(f32[2,2,4,128,512]{3,2,1,0,4:T(4,128)} %copy.59), channel_id=1, replica_groups=mesh['row'=4,'col'=8] {'col'}, dimensions={4} | all-to-all | bytes 8388608 | tf_op jit(solution)/shard_map/all_to_all | solution.py:59
  1379.8 1.3 copy.60
  1381.1 1.7 fusion.78
  1382.9 1.2 copy.62
  1384.1 1.5 squeeze.5
  1385.6 2.8 copy.61
  1388.4 1.5 squeeze.4
  1389.8 0.0 copy-start.3
  1389.8 13.4 fusion.7
  1403.3 0.0 copy-done.3
  1403.3 12.0 fusion.33
  1415.3 1.1 copy.63
  1416.4 2.0 reshape.20
  1418.4 28.1 %all_to_all.109 = f32[4,1,65536]{2,1,0:T(1,128)S(1)} all-to-all(f32[4,1,65536]{2,1,0:T(1,128)S(1)} %reshape.20), channel_id=1, replica_groups=mesh['row'=4,'col'=8] {'row'}, dimensions={0} | all-to-all | bytes 2097152 | tf_op jit(solution)/shard_map/all_to_all | solution.py:64
  1446.6 3.7 reduce.1
  1450.3 2.8 reshape.21
  1453.1 0.0 copy-start
  1453.1 1.9 copy.64
  1455.0 0.0 copy-done
  1455.0 0.4 multiply_reduce_fusion
  1455.4 37.8 %all-reduce = (f32[2]{0:T(128)S(1)}, f32[2]{0:T(128)S(1)}) all-reduce(f32[2]{0:T(128)S(1)} %get-tuple-element.3, f32[2]{0:T(128)S(1)} %get-tuple-element.2), channel_id=1, replica_groups=mesh['row'=4,'col'=8] {'row','col'}, use_global_device_ids=true, to_apply=%region_1.2 | all-reduce | flops 4 | bytes 32 | tf_op jit(solution)/shard_map/psum | solution.py:21
  1493.3 1.6 multiply_subtract_fusion
  (1 shorter events, 0.0 us)
Async XLA Ops:
  170.1 38.8 %copy-start.2 = (f32[2,2,4,8,128,64]{4,5,3,2,1,0:T(8,128)S(1)}, f32[2,2,4,8,128,64]{4,5,3,2,1,0:T(8,128)}, u32[]{:S(2)}) copy-start(f32[2,2,4,8,128,64]{4,5,3,2,1,0:T(8,128)} %copy.73) | copy-start | bytes 12582916
  272.1 188.4 %all-to-all-start.2 = ((f32[2,2,4,128,1024]{3,2,1,0,4:T(4,128)}), f32[2,2,4,128,1024]{3,2,1,0,4:T(4,128)}, u32[]{:S(2)}, u32[]{:S(2)}) async-start(f32[2,2,4,128,1024]{3,2,1,0,4:T(4,128)} %copy.50), calls=%async_computation.2 | async-start | bytes 16777216 | tf_op jit(solution)/shard_map/all_to_all | solution.py:53
  1243.1 52.5 %copy-start.1 = (f32[2,2,4,128,1024]{4,3,2,1,0:T(8,128)S(1)}, f32[2,2,4,128,1024]{4,3,2,1,0:T(8,128)}, u32[]{:S(2)}) copy-start(f32[2,2,4,128,1024]{4,3,2,1,0:T(8,128)} %all_to_all.91) | copy-start | bytes 25165828
  1389.8 13.4 copy-start.3
  1453.1 2.0 copy-start
where the time goes:
time: 1510 us; the launch traced here: 1500 us
  matrix products  644 us (43%)
  blocking collectives  395 us (26%)
  local copies, waits for them, and re-layouts  383 us (25%)
  other arithmetic  42 us (3%)
  waiting for transfers between devices  24.8 us (2%)
    dot_general x1, matrix products, local(): jnp.einsum('uvst,rktuv->rksuv', blocks, all_segments, precision=precise)  444 us
    all_to_all x1, blocking collectives, local(): lax.all_to_all(mixture, 'row', split_axis=2, concat_axis=4, tiled=True)  190 us
    reshape x1, local copies, waits for them, and re-layouts, local(): symbol.reshape(symbol.shape[0], symbol.shape[1], seg_count, seg_count)  124 us
    all_to_all x3, local copies, waits for them, and re-layouts, local(): lax.all_to_all(spectrum, 'row', split_axis=4, concat_axis=2, tiled=True)  71.6 us
    unnamed x14, local copies, waits for them, and re-layouts  62.3 us
    transpose x1, local copies, waits for them, and re-layouts, local(): jnp.einsum('uvst,rktuv->rksuv', blocks, all_segments, precision=precise)  54.4 us
    all_to_all x1, blocking collectives, local(): lax.all_to_all(jnp.stack([real_rows, imag_rows]), 'col', split_axis=3, co...  53.7 us
    all_to_all x1, blocking collectives, local(): lax.all_to_all(inverted, 'col', split_axis=4, concat_axis=3, tiled=True)  52.9 us
  transfers between devices with their start and end apart: 1, of which 1 were waited for; matrix products, arithmetic and copies ran while one was open for 11% of the time, Pallas kernels for 0%

commit v1 on v0

--- a/solution.py
+++ b/solution.py
@@ -44,8 +44,14 @@
     whole_rows = lax.all_to_all(right_side, "row", split_axis=1, concat_axis=2, tiled=True)
     real_rows = jnp.einsum("ui,ksij->ksuj", rows_cos, whole_rows, precision=precise)
     imag_rows = -jnp.einsum("ui,ksij->ksuj", rows_sin, whole_rows, precision=precise)
-    whole_cols = lax.all_to_all(
-        jnp.stack([real_rows, imag_rows]), "col", split_axis=3, concat_axis=4, tiled=True
+    whole_cols = jnp.concatenate(
+        lax.all_to_all(
+            jnp.stack(jnp.split(jnp.stack([real_rows, imag_rows]), lax.axis_size("col"), axis=3)),
+            "col",
+            0,
+            0,
+        ),
+        axis=4,
     )
     cos_part = jnp.einsum("vj,rksuj->rksuv", cols_cos, whole_cols, precision=precise)
     sin_part = jnp.einsum("vj,rksuj->rksuv", cols_sin, whole_cols, precision=precise)

time: 1510 us -> 1460 us (0.967)
  local copies, waits for them, and re-layouts: 383 us -> 342 us
  other arithmetic: 42 us -> 26.5 us
    unnamed x14 -> x10, local copies, waits for them, and re-layouts: 62.3 us -> 39.6 us
where the time goes in v1:
time: 1460 us; the launch traced here: 1450 us
  matrix products  655 us (45%)
  blocking collectives  393 us (27%)
  local copies, waits for them, and re-layouts  342 us (23%)
  other arithmetic  26.5 us (2%)
  waiting for transfers between devices  24.9 us (2%)
    dot_general x1, matrix products, local(): jnp.einsum('uvst,rktuv->rksuv', blocks, all_segments, precision=precise)  444 us
    all_to_all x1, blocking collectives, local(): lax.all_to_all(mixture, 'row', split_axis=2, concat_axis=4, tiled=True)  190 us
    reshape x1, local copies, waits for them, and re-layouts, local(): symbol.reshape(symbol.shape[0], symbol.shape[1], seg_count, seg_count)  124 us
    all_to_all x3, local copies, waits for them, and re-layouts, local(): lax.all_to_all(spectrum, 'row', split_axis=4, concat_axis=2, tiled=True)  71.6 us
    transpose x1, local copies, waits for them, and re-layouts, local(): jnp.einsum('uvst,rktuv->rksuv', blocks, all_segments, precision=precise)  54.4 us
    all_to_all x1, blocking collectives, local(): lax.all_to_all(inverted, 'col', split_axis=4, concat_axis=3, tiled=True)  52.9 us
    all_to_all x1, blocking collectives, local(): lax.all_to_all(jnp.stack(jnp.split(jnp.stack([real_rows, imag_rows]), lax...  52.6 us
    dot_general x1, matrix products, local(): jnp.einsum('jv,rksuv->rksuj', back_cols_sin, own_segments, precision=prec...  52.4 us
  transfers between devices with their start and end apart: 1, of which 1 were waited for; matrix products, arithmetic and copies ran while one was open for 11% of the time, Pallas kernels for 0%

profile of v1, /device:TPU:0, one launch (start us, length us, event | category | flops | bytes accessed | tf_op | source)
XLA Modules:
  0.0 1449.4 jit_solution(6859956753004009674)
XLA Ops:
  0.6 1.3 copy.42
  2.0 31.9 %all_to_all.92 = f32[2,16,128,64]{2,3,0,1:T(8,128)S(1)} all-to-all(f32[2,16,128,64]{2,3,0,1:T(8,128)S(1)} %copy.42), channel_id=1, replica_groups=mesh['row'=4,'col'=8] {'row'}, dimensions={1} | all-to-all | bytes 2097152 | tf_op jit(solution)/shard_map/all_to_all | solution.py:44
  33.8 0.7 copy.73
  34.5 0.4 all_to_all.69
  34.9 12.7 fusion.24
  47.7 12.5 negate_bitcast_fusion
  60.2 0.1 fusion.51
  60.3 0.1 fusion.54
  60.3 0.1 fusion.57
  60.4 0.1 fusion.60
  60.5 0.1 fusion.63
  60.6 0.1 fusion.66
  60.7 0.1 fusion.48
  60.7 0.1 fusion.68
  60.8 52.6 %all_to_all.93 = f32[8,2,2,4,128,64]{4,5,3,2,1,0:T(8,128)S(1)} all-to-all(f32[8,2,2,4,128,64]{4,5,3,2,1,0:T(8,128)S(1)} %fusion.68), channel_id=1, replica_groups=mesh['row'=4,'col'=8] {'col'}, dimensions={0} | all-to-all | bytes 8388608 | tf_op jit(solution)/shard_map/all_to_all | solution.py:48
  113.4 0.6 copy.44
  114.0 48.0 %fusion.17 = f32[2,2,4,128,1024]{4,3,2,1,0:T(8,128)} fusion(f32[2,2,4,128,512]{3,4,2,1,0:T(8,128)S(1)} %bitcast.137), kind=kOutput, calls=%fused_computation.41 | convolution fusion | flops 12892241920 | bytes 12582912 | tf_op jit(solution)/shard_map/vj,rksuj->rksuv/dot_general | solution.py:57
  162.0 36.0 %fusion.5 = f32[2,2,4,128,1024]{4,3,2,1,0:T(8,128)} fusion(f32[2,2,4,128,512]{3,4,2,1,0:T(8,128)S(1)} %bitcast.138), kind=kOutput, calls=%fused_computation.29 | convolution fusion | flops 12892241920 | bytes 12582912 | tf_op jit(solution)/shard_map/vj,rksuj->rksuv/dot_general | solution.py:56
  198.0 10.3 slice_add_fusion
  208.3 6.7 pad_maximum_fusion
  214.9 10.2 copy.47
  225.2 5.6 all-to-all-start.2
  230.8 33.5 %copy.50 = f32[128,256,256]{1,2,0:T(8,128)} copy(f32[128,256,256]{2,1,0:T(8,128)} %param.3) | data formatting | bytes 67108864 | tf_op args[1]
  264.2 124.5 %copy.68 = f32[128,256,16,16,1]{3,2,4,1,0:T(8,128)} copy(f32[128,256,16,16,1]{1,3,2,0,4:T(8,128)} %bitcast.127) | data formatting | bytes 67108864 | tf_op jit(solution)/shard_map/reshape | solution.py:32
  388.7 24.9 %all-to-all-done.2 = f32[2,2,4,128,1024]{3,2,1,0,4:T(4,128)} async-done(((f32[2,2,4,128,1024]{3,2,1,0,4:T(4,128)}), f32[2,2,4,128,1024]{3,2,1,0,4:T(4,128)}, u32[]{:S(2)}, u32[]{:S(2)}) %all-to-all-start.2) | async-done | bytes 8388640 | tf_op jit(solution)/shard_map/all_to_all | solution.py:59
  413.6 9.3 copy.48
  422.9 9.9 copy.49
  432.8 52.4 %copy.51 = f32[2,2,16,128,256]{2,1,0,4,3:T(2,128)} copy(f32[2,2,16,128,256]{4,3,2,1,0:T(8,128)} %bitcast.128) | data formatting | bytes 16777216 | tf_op jit(solution)/shard_map/all_to_all | solution.py:59
  485.2 443.6 %convolution_bitcast_fusion = f32[2,2,16,128,256]{2,1,0,4,3:T(2,128)} fusion(f32[2,2,16,128,256]{2,1,0,4,3:T(2,128)} %copy.51, f32[128,256,16,16,1]{3,2,4,1,0:T(8,128)} %copy.68), kind=kOutput, calls=%fused_computation | convolution fusion | flops 402653184 | bytes 50331648 | tf_op jit(solution)/shard_map/uvst,rktuv->rksuv/dot_general | solution.py:60
  928.8 54.4 %copy.53 = f32[2,2,16,128,256]{4,3,1,0,2:T(8,128)} copy(f32[2,2,16,128,256]{2,1,0,4,3:T(2,128)} %convolution_bitcast_fusion) | data formatting | bytes 16777216 | tf_op jit(solution)/shard_map/uvst,rktuv->rksuv/transpose | solution.py:60
  983.1 190.1 %all_to_all.94 = f32[2,2,16,128,256]{4,3,1,0,2:T(8,128)} all-to-all(f32[2,2,16,128,256]{4,3,1,0,2:T(8,128)} %copy.53), channel_id=1, replica_groups=mesh['row'=4,'col'=8] {'row'}, dimensions={2} | all-to-all | bytes 16777216 | tf_op jit(solution)/shard_map/all_to_all | solution.py:61
  1173.2 12.2 copy.55
  1185.4 10.7 all_to_all.78
  1196.2 0.0 copy-start.1
  1196.2 52.4 %fusion.15 = f32[2,2,4,128,512]{4,3,2,1,0:T(8,128)S(1)} fusion(f32[2,2,4,128,1024]{4,3,2,1,0:T(8,128)} %all_to_all.78), kind=kOutput, calls=%fused_computation.39 | convolution fusion | flops 12892241920 | bytes 12582912 | tf_op jit(solution)/shard_map/jv,rksuv->rksuj/dot_general | solution.py:63
  1248.6 0.0 copy-done.1
  1248.6 22.5 %fusion.3 = f32[2,2,4,128,512]{4,3,2,1,0:T(8,128)S(1)} fusion(f32[2,2,4,128,1024]{4,3,2,1,0:T(8,128)S(1)} %copy-done.1), kind=kOutput, calls=%fused_computation.27 | convolution fusion | flops 12892241920 | bytes 12582912 | tf_op jit(solution)/shard_map/jv,rksuv->rksuj/dot_general | solution.py:62
  1271.2 1.0 slice_subtract_fusion.1
  1272.2 2.4 pad_maximum_fusion.1
  1274.5 5.4 copy.56
  1280.0 52.9 %all_to_all.95 = f32[2,2,4,128,512]{3,2,1,0,4:T(4,128)S(1)} all-to-all(f32[2,2,4,128,512]{3,2,1,0,4:T(4,128)} %copy.56), channel_id=1, replica_groups=mesh['row'=4,'col'=8] {'col'}, dimensions={4} | all-to-all | bytes 8388608 | tf_op jit(solution)/shard_map/all_to_all | solution.py:65
  1332.8 1.3 copy.57
  1334.2 1.8 fusion.101
  1336.0 1.2 copy.58
  1337.2 1.5 squeeze.4
  1338.7 0.0 copy-start.2
  1338.7 13.7 fusion.7
  1352.4 0.0 copy-done.2
  1352.4 1.2 copy.59
  1353.6 1.5 squeeze.5
  1355.1 13.7 fusion.33
  1368.8 1.1 copy.60
  1370.0 2.0 reshape.26
  1372.0 28.1 %all_to_all.96 = f32[4,1,65536]{2,1,0:T(1,128)S(1)} all-to-all(f32[4,1,65536]{2,1,0:T(1,128)S(1)} %reshape.26), channel_id=1, replica_groups=mesh['row'=4,'col'=8] {'row'}, dimensions={0} | all-to-all | bytes 2097152 | tf_op jit(solution)/shard_map/all_to_all | solution.py:70
  1400.1 0.5 broadcast.73
  1400.6 3.7 reduce
  1404.3 2.8 reshape.27
  1407.1 0.0 copy-start
  1407.1 1.9 copy.61
  1409.1 0.0 copy-done
  1409.1 0.4 multiply_reduce_fusion
  1409.5 37.8 %all-reduce = (f32[2]{0:T(128)S(1)}, f32[2]{0:T(128)S(1)}) all-reduce(f32[2]{0:T(128)S(1)} %get-tuple-element.3, f32[2]{0:T(128)S(1)} %get-tuple-element.2), channel_id=1, replica_groups=mesh['row'=4,'col'=8] {'row','col'}, use_global_device_ids=true, to_apply=%region_1.2 | all-reduce | flops 4 | bytes 32 | tf_op jit(solution)/shard_map/psum | solution.py:21
  1447.3 1.6 multiply_subtract_fusion
  (1 shorter events, 0.0 us)
Async XLA Ops:
  225.2 188.4 %all-to-all-start.2 = ((f32[2,2,4,128,1024]{3,2,1,0,4:T(4,128)}), f32[2,2,4,128,1024]{3,2,1,0,4:T(4,128)}, u32[]{:S(2)}, u32[]{:S(2)}) async-start(f32[2,2,4,128,1024]{3,2,1,0,4:T(4,128)} %copy.47), calls=%async_computation.2 | async-start | bytes 16777216 | tf_op jit(solution)/shard_map/all_to_all | solution.py:59
  1196.2 52.5 %copy-start.1 = (f32[2,2,4,128,1024]{4,3,2,1,0:T(8,128)S(1)}, f32[2,2,4,128,1024]{4,3,2,1,0:T(8,128)}, u32[]{:S(2)}) copy-start(f32[2,2,4,128,1024]{4,3,2,1,0:T(8,128)} %all_to_all.78) | copy-start | bytes 25165828
  1338.7 13.7 copy-start.2
  1407.1 2.0 copy-start
